TPU v7x, 32 devices: a whole 2x2x4 slice. The times are simulated.
32 devices in a mesh: dp: 8 (over z, y), tensor: 4 (over x, core).
Axes of the slice: x: 2, y: 2, z: 4, core: 2. Of those that a mesh axis runs over, the one named last changes fastest.
Arguments:
- signal: bfloat16 [26112, 512], P('dp', 'tensor'), may hold values from -6 to 6
- horizon: int32 [32], P('dp'), may hold values from 96 to 720, as said below
- down_a: bfloat16 [6144, 512], P('dp', 'tensor'), may hold values from -0.078125 to 0.078125
- iso_a: bfloat16 [34816, 512], P('dp', 'tensor'), may hold values from -0.046875 to 0.046875
- up_a: bfloat16 [512, 12, 512], P('dp', None, 'tensor'), may hold values from -0.25 to 0.25
- down_b: bfloat16 [8192, 512], P('dp', 'tensor'), may hold values from -0.0625 to 0.0625
- iso_b: bfloat16 [26112, 512], P('dp', 'tensor'), may hold values from -0.0546875 to 0.0546875
- up_b: bfloat16 [512, 16, 512], P('dp', None, 'tensor'), may hold values from -0.25 to 0.25
- merge_w: bfloat16 [1024, 512], P('dp', 'tensor'), may hold values from -0.1875 to 0.1875
- ff_in: bfloat16 [512, 2048], P(None, 'tensor'), may hold values from -0.25 to 0.25
- ff_out: bfloat16 [2048, 512], P('tensor'), may hold values from -0.125 to 0.125
- norm_gain: float32 [512], P('tensor'), may hold values from 0.1 to 1.9
- norm_bias: float32 [512], P('tensor'), may hold values from -4 to 4
- first_gain: float32 [512], P('tensor'), may hold values from 0.1 to 1.9
- first_bias: float32 [512], P('tensor'), may hold values from -4 to 4
- last_gain: float32 [512], P('tensor'), may hold values from 0.1 to 1.9
- last_bias: float32 [512], P('tensor'), may hold values from -4 to 4
- cotangent: bfloat16 [26112, 512], P('dp', 'tensor'), may hold values from -6 to 6
Outputs:
- series_out: bfloat16 [26112, 512], P('dp', 'tensor')
- grad_input: float32 [26112, 512], P('dp', 'tensor')
- grad_down_a: float32 [6144, 512], P('dp', 'tensor')
- grad_iso_a: float32 [34816, 512], P('dp', 'tensor')
- grad_up_a: float32 [512, 12, 512], P('dp', None, 'tensor')
- grad_down_b: float32 [8192, 512], P('dp', 'tensor')
- grad_iso_b: float32 [26112, 512], P('dp', 'tensor')
- grad_up_b: float32 [512, 16, 512], P('dp', None, 'tensor')
- grad_merge: float32 [1024, 512], P('dp', 'tensor')
- grad_ff_in: float32 [512, 2048], P(None, 'tensor')
- grad_ff_out: float32 [2048, 512], P('tensor')
- grad_norm_gain: float32 [512], P('tensor')
- grad_norm_bias: float32 [512], P('tensor')
- grad_first_gain: float32 [512], P('tensor')
- grad_first_bias: float32 [512], P('tensor')
- grad_last_gain: float32 [512], P('tensor')
- grad_last_bias: float32 [512], P('tensor')
Inputs may be any that keep to these rules, and one draw needn't show every extreme that they name: Each series' horizon is one of 96, 192, 336 and 720; some series has 720.
All inputs are finite; a program needn't handle non-finite values.
Results may differ from a plain program's by a relative error of at most 0.014.
Values may be sent and summed in bfloat16 or wider, within the bound.
No kernel may reach another device: no remote copies, remote signals or barrier semaphores. Data moves between devices by JAX's collectives and lax.ppermute only.
A program may use at most 384 MiB of HBM per device.

v0:
```python
from functools import partial
import jax
import jax.numpy as jnp
from jax import lax
from jax.sharding import PartitionSpec as P

D = 512
SA = 12
SB = 16
IN_LEN = 96
L = 816
MA = 68
MB = 51
EPS = 1e-05


def channel_gather(operand):
    return lax.all_gather(operand, "tensor", axis=1, tiled=True)


def channel_sum(operand):
    return lax.psum_scatter(operand, "tensor", scatter_dimension=1, tiled=True)


def row_totals(first, second):
    return lax.psum((first, second), "tensor")


def matmul(left, right):
    return jnp.dot(left, right, preferred_element_type=jnp.float32)


def over_rows(left, right):
    return lax.dot_general(
        left, right, (((0,), (0,)), ((), ())), preferred_element_type=jnp.float32
    )


def against(left, right):
    return lax.dot_general(
        left, right, (((1,), (1,)), ((), ())), preferred_element_type=jnp.float32
    )


def norm_forward(operand, gain_vec, bias_vec):
    row_total, row_square = row_totals(
        jnp.sum(operand, axis=1, keepdims=True), jnp.sum(operand * operand, axis=1, keepdims=True)
    )
    row_mean = row_total / D
    inv_std = lax.rsqrt(row_square / D - row_mean * row_mean + EPS)
    normed = (operand - row_mean) * inv_std
    return (normed * gain_vec + bias_vec, (normed, inv_std))


def norm_backward(upstream, gain_vec, stored):
    normed, inv_std = stored
    scaled = upstream * gain_vec
    first_sum, second_sum = row_totals(
        jnp.sum(scaled, axis=1, keepdims=True), jnp.sum(scaled * normed, axis=1, keepdims=True)
    )
    result = inv_std * (scaled - first_sum / D - normed * second_sum / D)
    return (result, jnp.sum(upstream * normed, axis=0), jnp.sum(upstream, axis=0))


def unfold(sequence, span_len):
    padded = jnp.pad(sequence, ((0, 0), (span_len - 1, 0), (0, 0)))
    return jnp.concatenate(
        [padded[:, offset : offset + span_len, :] for offset in range(span_len)], axis=2
    )


def fold(windows, series_count, span_len):
    zeros_in = jnp.zeros((series_count, span_len, D), jnp.float32)
    _, back = jax.vjp(lambda seq_in: unfold(seq_in, span_len), zeros_in)
    return back(windows)[0]


def body(
    signal,
    horizon,
    down_a,
    iso_a,
    up_a,
    down_b,
    iso_b,
    up_b,
    merge_w,
    ff_in,
    ff_out,
    norm_gain,
    norm_bias,
    first_gain,
    first_bias,
    last_gain,
    last_bias,
    cotangent,
):
    row_count = signal.shape[0]
    col_count = signal.shape[1]
    series_count = row_count // L
    short_a = row_count // SA
    short_b = row_count // SB
    wd_a, wi_a, wu_a, wd_b, wi_b, wu_b, w_merge = (
        lax.all_gather(down_a, "dp", axis=0, tiled=True),
        lax.all_gather(iso_a, "dp", axis=0, tiled=True),
        lax.all_gather(up_a, "dp", axis=0, tiled=True),
        lax.all_gather(down_b, "dp", axis=0, tiled=True),
        lax.all_gather(iso_b, "dp", axis=0, tiled=True),
        lax.all_gather(up_b, "dp", axis=0, tiled=True),
        lax.all_gather(merge_w, "dp", axis=0, tiled=True),
    )
    x_full = channel_gather(signal)
    x_float = signal.astype(jnp.float32)
    window_a = x_full.reshape(short_a, SA * D)
    window_b = x_full.reshape(short_b, SB * D)
    down_act_a = jnp.tanh(matmul(window_a, wd_a))
    down_act_b = jnp.tanh(matmul(window_b, wd_b))
    down_low_a = down_act_a.astype(jnp.bfloat16)
    down_low_b = down_act_b.astype(jnp.bfloat16)
    down_full = channel_gather(jnp.concatenate([down_low_a, down_low_b], axis=0))
    taps_a = unfold(down_full[:short_a].reshape(series_count, MA, D), MA).reshape(short_a, MA * D)
    taps_b = unfold(down_full[short_a:].reshape(series_count, MB, D), MB).reshape(short_b, MB * D)
    iso_act_a = jnp.tanh(matmul(taps_a, wi_a))
    iso_act_b = jnp.tanh(matmul(taps_b, wi_b))
    middle_a, store_mid_a = norm_forward(
        iso_act_a + down_low_a.astype(jnp.float32), norm_gain, norm_bias
    )
    middle_b, store_mid_b = norm_forward(
        iso_act_b + down_low_b.astype(jnp.float32), norm_gain, norm_bias
    )
    middle_full = channel_gather(jnp.concatenate([middle_a, middle_b], axis=0).astype(jnp.bfloat16))
    mid_full_a = middle_full[:short_a]
    mid_full_b = middle_full[short_a:]
    up_act_a = jnp.tanh(
        matmul(mid_full_a, wu_a.reshape(D, SA * col_count)).reshape(row_count, col_count)
    )
    up_act_b = jnp.tanh(
        matmul(mid_full_b, wu_b.reshape(D, SB * col_count)).reshape(row_count, col_count)
    )
    branch_a, store_br_a = norm_forward(up_act_a + x_float, norm_gain, norm_bias)
    branch_b, store_br_b = norm_forward(up_act_b + x_float, norm_gain, norm_bias)
    pair_full = channel_gather(jnp.concatenate([branch_a, branch_b], axis=0).astype(jnp.bfloat16))
    merge_in = jnp.concatenate([pair_full[:row_count], pair_full[row_count:]], axis=1)
    merged = matmul(merge_in, w_merge)
    first_out, store_first = norm_forward(merged, first_gain, first_bias)
    first_full = channel_gather(first_out.astype(jnp.bfloat16))
    hidden_pre = matmul(first_full, ff_in)
    hidden = jax.nn.gelu(hidden_pre, approximate=False).astype(jnp.bfloat16)
    feed = channel_sum(matmul(hidden, ff_out))
    last_out, store_last = norm_forward(merged + feed, last_gain, last_bias)
    positions = lax.broadcasted_iota(jnp.int32, (series_count, L), 1)
    out_mask = (positions < IN_LEN + horizon[:, None]).astype(jnp.float32).reshape(row_count, 1)
    series_out = (last_out * out_mask).astype(jnp.bfloat16)
    upstream = cotangent.astype(jnp.float32) * out_mask
    grad_sum, grad_last_gain, grad_last_bias = norm_backward(upstream, last_gain, store_last)
    grad_feed = channel_gather(grad_sum.astype(jnp.bfloat16))
    grad_ff_out = over_rows(hidden, grad_feed)
    grad_hidden = against(grad_feed, ff_out)
    _, gelu_back = jax.vjp(partial(jax.nn.gelu, approximate=False), hidden_pre)
    grad_hpre = gelu_back(grad_hidden)[0].astype(jnp.bfloat16)
    grad_ff_in = over_rows(first_full, grad_hpre)
    grad_first = channel_sum(against(grad_hpre, ff_in))
    grad_merged_norm, grad_first_gain, grad_first_bias = norm_backward(
        grad_first, first_gain, store_first
    )
    grad_merged = (grad_merged_norm + grad_sum).astype(jnp.bfloat16)
    grad_merge = over_rows(merge_in, grad_merged)
    grad_pair_full = against(grad_merged, w_merge)
    grad_pair = channel_sum(jnp.concatenate([grad_pair_full[:, :D], grad_pair_full[:, D:]], axis=0))
    grad_resid_a, gain_part_one, bias_part_one = norm_backward(
        grad_pair[:row_count], norm_gain, store_br_a
    )
    grad_resid_b, gain_part_two, bias_part_two = norm_backward(
        grad_pair[row_count:], norm_gain, store_br_b
    )
    grad_upre_a = (
        (grad_resid_a * (1.0 - up_act_a * up_act_a))
        .astype(jnp.bfloat16)
        .reshape(short_a, SA * col_count)
    )
    grad_upre_b = (
        (grad_resid_b * (1.0 - up_act_b * up_act_b))
        .astype(jnp.bfloat16)
        .reshape(short_b, SB * col_count)
    )
    grad_up_a = over_rows(mid_full_a, grad_upre_a).reshape(D, SA, col_count)
    grad_up_b = over_rows(mid_full_b, grad_upre_b).reshape(D, SB, col_count)
    grad_mid_full_a = against(grad_upre_a, wu_a.reshape(D, SA * col_count))
    grad_mid_full_b = against(grad_upre_b, wu_b.reshape(D, SB * col_count))
    grad_middle = channel_sum(jnp.concatenate([grad_mid_full_a, grad_mid_full_b], axis=0))
    grad_inner_a, gain_part_three, bias_part_three = norm_backward(
        grad_middle[:short_a], norm_gain, store_mid_a
    )
    grad_inner_b, gain_part_four, bias_part_four = norm_backward(
        grad_middle[short_a:], norm_gain, store_mid_b
    )
    grad_ipre_a = (grad_inner_a * (1.0 - iso_act_a * iso_act_a)).astype(jnp.bfloat16)
    grad_ipre_b = (grad_inner_b * (1.0 - iso_act_b * iso_act_b)).astype(jnp.bfloat16)
    grad_iso_a = over_rows(taps_a, grad_ipre_a)
    grad_iso_b = over_rows(taps_b, grad_ipre_b)
    grad_taps_a = fold(
        against(grad_ipre_a, wi_a).reshape(series_count, MA, MA * D), series_count, MA
    ).reshape(short_a, D)
    grad_taps_b = fold(
        against(grad_ipre_b, wi_b).reshape(series_count, MB, MB * D), series_count, MB
    ).reshape(short_b, D)
    grad_down = channel_sum(jnp.concatenate([grad_taps_a, grad_taps_b], axis=0))
    grad_dpre_a = ((grad_down[:short_a] + grad_inner_a) * (1.0 - down_act_a * down_act_a)).astype(
        jnp.bfloat16
    )
    grad_dpre_b = ((grad_down[short_a:] + grad_inner_b) * (1.0 - down_act_b * down_act_b)).astype(
        jnp.bfloat16
    )
    grad_down_a = over_rows(window_a, grad_dpre_a)
    grad_down_b = over_rows(window_b, grad_dpre_b)
    grad_x_full = against(grad_dpre_a, wd_a).reshape(row_count, D) + against(
        grad_dpre_b, wd_b
    ).reshape(row_count, D)
    grad_input = channel_sum(grad_x_full) + grad_resid_a + grad_resid_b
    sum_down_a, sum_iso_a, sum_up_a, sum_down_b, sum_iso_b, sum_up_b, sum_merge = (
        lax.psum_scatter(grad_down_a, "dp", scatter_dimension=0, tiled=True),
        lax.psum_scatter(grad_iso_a, "dp", scatter_dimension=0, tiled=True),
        lax.psum_scatter(grad_up_a, "dp", scatter_dimension=0, tiled=True),
        lax.psum_scatter(grad_down_b, "dp", scatter_dimension=0, tiled=True),
        lax.psum_scatter(grad_iso_b, "dp", scatter_dimension=0, tiled=True),
        lax.psum_scatter(grad_up_b, "dp", scatter_dimension=0, tiled=True),
        lax.psum_scatter(grad_merge, "dp", scatter_dimension=0, tiled=True),
    )
    grad_norm_gain = gain_part_one + gain_part_two + gain_part_three + gain_part_four
    grad_norm_bias = bias_part_one + bias_part_two + bias_part_three + bias_part_four
    (
        sum_ff_in,
        sum_ff_out,
        sum_norm_gain,
        sum_norm_bias,
        sum_first_gain,
        sum_first_bias,
        sum_last_gain,
        sum_last_bias,
    ) = lax.psum(
        (
            grad_ff_in,
            grad_ff_out,
            grad_norm_gain,
            grad_norm_bias,
            grad_first_gain,
            grad_first_bias,
            grad_last_gain,
            grad_last_bias,
        ),
        "dp",
    )
    return (
        series_out,
        grad_input,
        sum_down_a,
        sum_iso_a,
        sum_up_a,
        sum_down_b,
        sum_iso_b,
        sum_up_b,
        sum_merge,
        sum_ff_in,
        sum_ff_out,
        sum_norm_gain,
        sum_norm_bias,
        sum_first_gain,
        sum_first_bias,
        sum_last_gain,
        sum_last_bias,
    )


def solution(mesh):
    in_specs = (
        P("dp", "tensor"),
        P("dp"),
        P("dp", "tensor"),
        P("dp", "tensor"),
        P("dp", None, "tensor"),
        P("dp", "tensor"),
        P("dp", "tensor"),
        P("dp", None, "tensor"),
        P("dp", "tensor"),
        P(None, "tensor"),
        P("tensor", None),
        P("tensor"),
        P("tensor"),
        P("tensor"),
        P("tensor"),
        P("tensor"),
        P("tensor"),
        P("dp", "tensor"),
    )
    out_specs = (
        P("dp", "tensor"),
        P("dp", "tensor"),
        P("dp", "tensor"),
        P("dp", "tensor"),
        P("dp", None, "tensor"),
        P("dp", "tensor"),
        P("dp", "tensor"),
        P("dp", None, "tensor"),
        P("dp", "tensor"),
        P(None, "tensor"),
        P("tensor", None),
        P("tensor"),
        P("tensor"),
        P("tensor"),
        P("tensor"),
        P("tensor"),
        P("tensor"),
    )
    return jax.shard_map(body, mesh=mesh, in_specs=in_specs, out_specs=out_specs, check_vma=False)
```

profile of v0, /device:TPU:0, one launch (start us, length us, event | category | flops | bytes accessed | tf_op | source)
XLA Modules:
  0.0 2445.4 jit_solution(7700934560776956939)
XLA Ops:
  12.0 45.2 %all-gather.21.cloned.1.call-done = bf16[512,12,128]{2,0,1:T(8,128)(2,1)} async-done(((bf16[64,12,128]{2,0,1:T(8,128)(2,1)}), bf16[512,12,128]{2,0,1:T(8,128)(2,1)}) %all-gather.21.cloned.1.call-update) | async-done | bytes 1572880 | tf_op jit(solution)/shard_map/all_gather | solution.py:106
  59.7 27.9 %all-gather.11.cloned.1.call-done = bf16[3264,512]{1,0:T(8,128)(2,1)} async-done(((bf16[3264,128]{1,0:T(8,128)(2,1)}), bf16[3264,512]{1,0:T(8,128)(2,1)}) %all-gather.11.cloned.1.call-update) | async-done | bytes 3342352 | tf_op jit(solution)/shard_map/all_gather | solution.py:18
  101.1 38.0 %all-gather.15.cloned.1.call-done = bf16[8192,128]{1,0:T(8,128)(2,1)} async-done(((bf16[1024,128]{1,0:T(8,128)(2,1)}), bf16[8192,128]{1,0:T(8,128)(2,1)}) %all-gather.15.cloned.1.call-update) | async-done | bytes 2097168 | tf_op jit(solution)/shard_map/all_gather | solution.py:107
  143.4 40.4 %all-gather.13.cloned.1.call-done = bf16[6144,128]{1,0:T(8,128)(2,1)} async-done(((bf16[768,128]{1,0:T(8,128)(2,1)}), bf16[6144,128]{1,0:T(8,128)(2,1)}) %all-gather.13.cloned.1.call-update) | async-done | bytes 1572880 | tf_op jit(solution)/shard_map/all_gather | solution.py:104
  586.2 32.9 %all_gather.49 = bf16[1024,128]{1,0:T(8,128)(2,1)} all-gather(bf16[128,128]{1,0:T(8,128)(2,1)S(1)} %copy-done.172), channel_id=1, replica_groups=mesh['dp'=8,'tensor'=4] {'dp'}, dimensions={0}, use_global_device_ids=true | all-gather | bytes 294912 | tf_op jit(solution)/shard_map/all_gather | solution.py:110
  655.5 31.2 %all-gather.27.cloned.1.call-done = bf16[3264,512]{1,0:T(8,128)(2,1)} async-done(((bf16[3264,128]{1,0:T(8,128)(2,1)}), bf16[3264,512]{1,0:T(8,128)(2,1)}) %all-gather.27.cloned.1.call-update) | async-done | bytes 3342352 | tf_op jit(solution)/shard_map/all_gather | solution.py:18
  686.7 18.5 multiply_convert_fusion
  712.0 60.9 %reduce-scatter.14.cloned.1.call-done = f32[3264,128]{1,0:T(8,128)} async-done(((f32[3264,512]{1,0:T(8,128)}), f32[3264,128]{1,0:T(8,128)}) %reduce-scatter.14.cloned.1.call-update) | async-done | bytes 1671184 | tf_op jit(solution)/shard_map/reduce_scatter | solution.py:22
  814.4 31.4 %all-gather.29.cloned.1.call-done = bf16[3264,512]{1,0:T(8,128)(2,1)} async-done(((bf16[3264,128]{1,0:T(8,128)(2,1)}), bf16[3264,512]{1,0:T(8,128)(2,1)}) %all-gather.29.cloned.1.call-update) | async-done | bytes 3342352 | tf_op jit(solution)/shard_map/all_gather | solution.py:18
  862.2 61.1 %reduce-scatter.16.cloned.1.call-done = f32[3264,128]{1,0:T(8,128)} async-done(((f32[3264,512]{1,0:T(8,128)}), f32[3264,128]{1,0:T(8,128)}) %reduce-scatter.16.cloned.1.call-update) | async-done | bytes 1671184 | tf_op jit(solution)/shard_map/reduce_scatter | solution.py:22
  977.6 105.6 %reduce-scatter.18.cloned.1.call-done = f32[6528,128]{1,0:T(8,128)} async-done(((f32[6528,512]{1,0:T(8,128)}), f32[6528,128]{1,0:T(8,128)}) %reduce-scatter.18.cloned.1.call-update) | async-done | bytes 3342352 | tf_op jit(solution)/shard_map/reduce_scatter | solution.py:22
  1117.3 25.8 %reduce-scatter.20.cloned.1.call-done = f32[476,128]{1,0:T(8,128)} async-done(((f32[476,512]{1,0:T(8,128)}), f32[476,128]{1,0:T(8,128)}) %reduce-scatter.20.cloned.1.call-update) | async-done | bytes 243728 | tf_op jit(solution)/shard_map/reduce_scatter | solution.py:22
  1165.9 17.5 reshape.245
  1219.7 30.3 %reshape.243 = f32[4,68,34816]{2,1,0:T(8,128)} reshape(f32[272,34816]{1,0:T(8,128)} %fusion.60) | data formatting | bytes 75759616 | tf_op jit(solution)/shard_map/reshape | solution.py:202
  1311.6 22.4 reduce-scatter.22.cloned.1.call-done
  1426.2 22.4 all-reduce.121
  1450.8 53.4 %reduce-scatter.26.cloned.1.call-done = f32[768,128]{0,1:T(8,128)} async-done(((f32[6144,128]{0,1:T(8,128)}), f32[768,128]{0,1:T(8,128)}) %reduce-scatter.26.cloned.1.call-update) | async-done | bytes 393232 | tf_op jit(solution)/shard_map/reduce_scatter | solution.py:221
  1506.0 89.6 %reduce-scatter.32.cloned.1.call-done = f32[1024,128]{0,1:T(8,128)} async-done(((f32[8192,128]{0,1:T(8,128)}), f32[1024,128]{0,1:T(8,128)}) %reduce-scatter.32.cloned.1.call-update) | async-done | bytes 524304 | tf_op jit(solution)/shard_map/reduce_scatter | solution.py:224
  1597.7 61.2 %reduce-scatter.24.cloned.1.call-done = f32[3264,128]{1,0:T(8,128)} async-done(((f32[3264,512]{1,0:T(8,128)}), f32[3264,128]{1,0:T(8,128)}) %reduce-scatter.24.cloned.1.call-update) | async-done | bytes 1671184 | tf_op jit(solution)/shard_map/reduce_scatter | solution.py:22
  1667.6 98.2 %all-reduce.133.cloned.1.call-done = (f32[512,512]{1,0:T(8,128)}, f32[512,512]{1,0:T(8,128)}) async-done(((f32[512,512]{1,0:T(8,128)}, f32[512,512]{1,0:T(8,128)}), (f32[512,512]{1,0:T(8,128)}, f32[512,512]{1,0:T(8,128)})) %all-reduce.133.cloned.1.call-update) | async-done | bytes 2097168 | tf_op jit(solution)/shard_map/psum | solution.py:240
  1765.8 66.0 %reduce-scatter.38.cloned.1.call-done = f32[128,128]{1,0:T(8,128)} async-done(((f32[1024,128]{1,0:T(8,128)}), f32[128,128]{1,0:T(8,128)}) %reduce-scatter.38.cloned.1.call-update) | async-done | bytes 65552 | tf_op jit(solution)/shard_map/reduce_scatter | solution.py:227
  1831.8 78.1 %reduce-scatter.30.cloned.1.call-done = f32[64,12,128]{2,0,1:T(8,128)} async-done(((f32[512,12,128]{2,0,1:T(8,128)}), f32[64,12,128]{2,0,1:T(8,128)}) %reduce-scatter.30.cloned.1.call-update) | async-done | bytes 393232 | tf_op jit(solution)/shard_map/reduce_scatter | solution.py:223
  1909.9 221.7 %reduce-scatter.34.cloned.1.call-done = f32[3264,128]{1,0:T(8,128)} async-done(((f32[26112,128]{1,0:T(8,128)}), f32[3264,128]{1,0:T(8,128)}) %reduce-scatter.34.cloned.1.call-update) | async-done | bytes 1671184 | tf_op jit(solution)/shard_map/reduce_scatter | solution.py:225
  2131.6 302.3 %reduce-scatter.28.cloned.1.call-done = f32[4352,128]{1,0:T(8,128)} async-done(((f32[34816,128]{1,0:T(8,128)}), f32[4352,128]{1,0:T(8,128)}) %reduce-scatter.28.cloned.1.call-update) | async-done | bytes 2228240 | tf_op jit(solution)/shard_map/reduce_scatter | solution.py:222
  (806 shorter events, 847.1 us)
Async XLA Ops:
  7.2 49.9 %all-gather.21.cloned.1.call-start = ((), (), s32[]{:S(2)}) async-start(), calls=%async_computation.18 | async-start | bytes 1769472 | tf_op jit(solution)/shard_map/all_gather | solution.py:106
  7.9 79.7 %all-gather.11.cloned.1.call-start = ((), (), s32[]{:S(2)}) async-start(), calls=%async_computation.13 | async-start | bytes 4177920 | tf_op jit(solution)/shard_map/all_gather | solution.py:18
  8.7 130.4 %all-gather.15.cloned.1.call-start = ((), (), s32[]{:S(2)}) async-start(), calls=%async_computation.15 | async-start | bytes 2359296 | tf_op jit(solution)/shard_map/all_gather | solution.py:107
  9.4 174.4 %all-gather.13.cloned.1.call-start = ((), (), s32[]{:S(2)}) async-start(), calls=%async_computation.14 | async-start | bytes 1769472 | tf_op jit(solution)/shard_map/all_gather | solution.py:104
  10.0 506.6 %all-gather.19.cloned.1.call-start = ((), (), s32[]{:S(2)}) async-start(), calls=%async_computation.17 | async-start | bytes 7520256 | tf_op jit(solution)/shard_map/all_gather | solution.py:108
  10.6 515.3 %all-gather.17.cloned.1.call-start = ((), (), s32[]{:S(2)}) async-start(), calls=%async_computation.16 | async-start | bytes 10027008 | tf_op jit(solution)/shard_map/all_gather | solution.py:105
  11.2 546.7 %all-gather.23.cloned.1.call-start = ((), (), s32[]{:S(2)}) async-start(), calls=%async_computation.19 | async-start | bytes 2359296 | tf_op jit(solution)/shard_map/all_gather | solution.py:109
  11.9 622.4 %all-gather.25.cloned.1.call-start = ((), (), s32[]{:S(2)}) async-start(), calls=%async_computation.20 | async-start | bytes 8355840 | tf_op jit(solution)/shard_map/all_gather | solution.py:18
  586.2 100.5 %all-gather.27.cloned.1.call-start = ((), (), s32[]{:S(2)}) async-start(), calls=%async_computation.21 | async-start | bytes 4177920 | tf_op jit(solution)/shard_map/all_gather | solution.py:18
  655.4 117.5 %reduce-scatter.14.cloned.1.call-start = ((), (), s32[]{:S(2)}) async-start(), calls=%async_computation.22 | async-start | bytes 8355840 | tf_op jit(solution)/shard_map/reduce_scatter | solution.py:22
  711.7 134.0 %all-gather.29.cloned.1.call-start = ((), (), s32[]{:S(2)}) async-start(), calls=%async_computation.23 | async-start | bytes 4177920 | tf_op jit(solution)/shard_map/all_gather | solution.py:18
  814.3 108.9 %reduce-scatter.16.cloned.1.call-start = ((), (), s32[]{:S(2)}) async-start(), calls=%async_computation.24 | async-start | bytes 8355840 | tf_op jit(solution)/shard_map/reduce_scatter | solution.py:22
  862.1 221.1 %reduce-scatter.18.cloned.1.call-start = ((), (), s32[]{:S(2)}) async-start(), calls=%async_computation.25 | async-start | bytes 16711680 | tf_op jit(solution)/shard_map/reduce_scatter | solution.py:22
  977.6 165.6 %reduce-scatter.20.cloned.1.call-start = ((), (), s32[]{:S(2)}) async-start(), calls=%async_computation.26 | async-start | bytes 1228800 | tf_op jit(solution)/shard_map/reduce_scatter | solution.py:22
  1117.3 216.8 %reduce-scatter.22.cloned.1.call-start = ((), (), s32[]{:S(2)}) async-start(), calls=%async_computation.27 | async-start | bytes 1228800 | tf_op jit(solution)/shard_map/reduce_scatter | solution.py:22
  1308.3 140.3 %reduce-scatter.36.cloned.1.call-start = ((), (), s32[]{:S(2)}) async-start(), calls=%async_computation.34 | async-start | bytes 4718592 | tf_op jit(solution)/shard_map/reduce_scatter | solution.py:226
  1311.4 192.7 %reduce-scatter.26.cloned.1.call-start = ((), (), s32[]{:S(2)}) async-start(), calls=%async_computation.29 | async-start | bytes 3538944 | tf_op jit(solution)/shard_map/reduce_scatter | solution.py:221
  1339.8 255.8 %reduce-scatter.32.cloned.1.call-start = ((), (), s32[]{:S(2)}) async-start(), calls=%async_computation.32 | async-start | bytes 4718592 | tf_op jit(solution)/shard_map/reduce_scatter | solution.py:224
  1345.9 313.0 %reduce-scatter.24.cloned.1.call-start = ((), (), s32[]{:S(2)}) async-start(), calls=%async_computation.28 | async-start | bytes 8355840 | tf_op jit(solution)/shard_map/reduce_scatter | solution.py:22
  1379.3 386.5 %all-reduce.133.cloned.1.call-start = ((), (), s32[]{:S(2)}) async-start(), calls=%async_computation.36 | async-start | bytes 4194304 | tf_op jit(solution)/shard_map/psum | solution.py:240
  1388.5 443.3 %reduce-scatter.38.cloned.1.call-start = ((), (), s32[]{:S(2)}) async-start(), calls=%async_computation.35 | async-start | bytes 589824 | tf_op jit(solution)/shard_map/reduce_scatter | solution.py:227
  1394.5 515.4 %reduce-scatter.30.cloned.1.call-start = ((), (), s32[]{:S(2)}) async-start(), calls=%async_computation.31 | async-start | bytes 3538944 | tf_op jit(solution)/shard_map/reduce_scatter | solution.py:223
  1397.3 734.3 %reduce-scatter.34.cloned.1.call-start = ((), (), s32[]{:S(2)}) async-start(), calls=%async_computation.33 | async-start | bytes 15040512 | tf_op jit(solution)/shard_map/reduce_scatter | solution.py:225
  1410.4 1023.5 %reduce-scatter.28.cloned.1.call-start = ((), (), s32[]{:S(2)}) async-start(), calls=%async_computation.30 | async-start | bytes 20054016 | tf_op jit(solution)/shard_map/reduce_scatter | solution.py:222
  (192 other events, 10077.3 us)
Sparse Core Ops, SparseCore 0:
  10.2 46.8 all-gather.20
  58.7 28.8 all-gather.10
  89.7 49.2 all-gather.14
  141.1 42.6 all-gather.12
  185.8 102.7 all-gather.18
  290.6 129.7 all-gather.16
  422.6 47.4 all-gather.22
  586.3 47.9 all-gather.24
  655.5 31.1 all-gather.26
  711.9 60.9 reduce-scatter.13
  814.5 31.2 all-gather.28
  862.2 60.9 reduce-scatter.15
  977.7 105.4 reduce-scatter.17
  1117.4 25.7 reduce-scatter.19
  1308.4 25.6 reduce-scatter.21
  1337.5 88.2 reduce-scatter.35
  1429.7 74.3 reduce-scatter.25
  1508.0 87.5 reduce-scatter.31
  1598.2 60.7 reduce-scatter.23
  1663.5 102.2 all-reduce.132
  1770.1 61.6 reduce-scatter.37
  1836.0 73.8 reduce-scatter.29
  1914.1 217.3 reduce-scatter.33
  2136.4 297.3 reduce-scatter.27
where the time goes:
time: 2460 us; the launch traced here: 2450 us
  waiting for transfers between devices  1480 us (60%)
  local copies, waits for them, and re-layouts  493 us (20%)
  matrix products  186 us (8%)
  blocking collectives  149 us (6%)
  other arithmetic  120 us (5%)
    reduce_scatter x6, waiting for transfers between devices, channel_sum(): return lax.psum_scatter(operand, 'tensor', scatter_dimension=1, tiled=True)  337 us
    reduce_scatter x1, waiting for transfers between devices, body(): lax.psum_scatter(grad_iso_a, 'dp', scatter_dimension=0, tiled=True)  302 us
    reduce_scatter x1, waiting for transfers between devices, body(): lax.psum_scatter(grad_iso_b, 'dp', scatter_dimension=0, tiled=True)  222 us
    concatenate x119, local copies, waits for them, and re-layouts, unfold(): jnp.concatenate([padded[:, offset:offset + span_len, :] for offset in ran...  191 us
    unnamed x507, local copies, waits for them, and re-layouts  133 us
    all_gather x4, waiting for transfers between devices, channel_gather(): return lax.all_gather(operand, 'tensor', axis=1, tiled=True)  106 us
    psum x1, waiting for transfers between devices, body(): lax.psum((grad_ff_in, grad_ff_out, grad_norm_gain, grad_norm_bias, grad_f...  98.2 us
    reduce_scatter x1, waiting for transfers between devices, body(): lax.psum_scatter(grad_down_b, 'dp', scatter_dimension=0, tiled=True)  89.6 us
  transfers between devices with their start and end apart: 24, of which 20 were waited for; matrix products, arithmetic and copies ran while one was open for 20% of the time, Pallas kernels for 0%

commit v1 on v0

--- a/solution.py
+++ b/solution.py
@@ -14,8 +14,24 @@
 EPS = 1e-05
 
 
+def ring_gather(x, axis, dim):
+    ways, here, step = (lax.axis_size(axis), lax.axis_index(axis), x.shape[dim])
+    shape = [n * ways if d == dim else n for d, n in enumerate(x.shape)]
+    full = lax.dynamic_update_slice_in_dim(jnp.zeros(shape, x.dtype), x, here * step, axis=dim)
+    going_up = going_down = x
+    for far in range(1, ways // 2 + 1):
+        going_up = lax.ppermute(going_up, axis, [(d, (d + 1) % ways) for d in range(ways)])
+        full = lax.dynamic_update_slice_in_dim(full, going_up, (here - far) % ways * step, axis=dim)
+        if 2 * far < ways:
+            going_down = lax.ppermute(going_down, axis, [(d, (d - 1) % ways) for d in range(ways)])
+            full = lax.dynamic_update_slice_in_dim(
+                full, going_down, (here + far) % ways * step, axis=dim
+            )
+    return full
+
+
 def channel_gather(operand):
-    return lax.all_gather(operand, "tensor", axis=1, tiled=True)
+    return ring_gather(operand, "tensor", 1)
 
 
 def channel_sum(operand):

time: 2460 us -> 2400 us (0.976)
  waiting for transfers between devices: 1480 us -> 1420 us
    ppermute x0 -> x18, waiting for transfers between devices: none -> 117 us  [the longest x12 117 us: ring_gather(): lax.ppermute(going_up, axis, [(d, (d + 1) % ways) for d in range(ways)])]
    all_gather x4 -> x0, waiting for transfers between devices: 106 us -> none  [channel_gather(): return lax.all_gather(operand, 'tensor', axis=1, tiled=True)]
    all_gather x1, waiting for transfers between devices: 45.2 us -> 0.01 us  [body(): lax.all_gather(up_a, 'dp', axis=0, tiled=True)]
    all_gather x1, waiting for transfers between devices: 40.4 us -> 1.45 us  [body(): lax.all_gather(down_a, 'dp', axis=0, tiled=True)]
    reduce_scatter x1, waiting for transfers between devices: 53.4 us -> 78.3 us  [body(): lax.psum_scatter(grad_down_a, 'dp', scatter_dimension=0, tiled=True)]
    unnamed x507 -> x513, local copies, waits for them, and re-layouts: 133 us -> 128 us
  transfers between devices with their start and end apart: 24 -> 38, of which waited for: 20 -> 27; matrix products, arithmetic and copies ran while one was open for 20% -> 20% of each run, Pallas kernels for 0% -> 0%
where the time goes in v1:
time: 2400 us; the launch traced here: 2390 us
  waiting for transfers between devices  1420 us (59%)
  local copies, waits for them, and re-layouts  496 us (21%)
  matrix products  183 us (8%)
  blocking collectives  131 us (5%)
  other arithmetic  117 us (5%)
    reduce_scatter x6, waiting for transfers between devices, channel_sum(): return lax.psum_scatter(operand, 'tensor', scatter_dimension=1, tiled=True)  319 us
    reduce_scatter x1, waiting for transfers between devices, body(): lax.psum_scatter(grad_iso_a, 'dp', scatter_dimension=0, tiled=True)  302 us
    reduce_scatter x1, waiting for transfers between devices, body(): lax.psum_scatter(grad_iso_b, 'dp', scatter_dimension=0, tiled=True)  222 us
    concatenate x119, local copies, waits for them, and re-layouts, unfold(): jnp.concatenate([padded[:, offset:offset + span_len, :] for offset in ran...  191 us
    unnamed x513, local copies, waits for them, and re-layouts  128 us
    ppermute x12, waiting for transfers between devices, ring_gather(): lax.ppermute(going_up, axis, [(d, (d + 1) % ways) for d in range(ways)])  117 us
    psum x1, waiting for transfers between devices, body(): lax.psum((grad_ff_in, grad_ff_out, grad_norm_gain, grad_norm_bias, grad_f...  97.6 us
    reduce_scatter x1, waiting for transfers between devices, body(): lax.psum_scatter(grad_down_b, 'dp', scatter_dimension=0, tiled=True)  91.7 us
  transfers between devices with their start and end apart: 38, of which 27 were waited for; matrix products, arithmetic and copies ran while one was open for 20% of the time, Pallas kernels for 0%

profile of v1, /device:TPU:0, one launch (start us, length us, event | category | flops | bytes accessed | tf_op | source)
XLA Modules:
  0.0 2390.2 jit_solution(1575661926001045654)
XLA Ops:
  61.3 46.1 %all-gather.9.cloned.1.call-done = bf16[8192,128]{1,0:T(8,128)(2,1)} async-done(((bf16[1024,128]{1,0:T(8,128)(2,1)}), bf16[8192,128]{1,0:T(8,128)(2,1)}) %all-gather.9.cloned.1.call-update) | async-done | bytes 2097168 | tf_op jit(solution)/shard_map/all_gather | solution.py:123
  514.7 34.4 %collective-permute-done.9 = bf16[6528,128]{1,0:T(8,128)(2,1)S(1)} collective-permute-done((bf16[6528,128]{1,0:T(8,128)(2,1)S(1)}, bf16[6528,128]{1,0:T(8,128)(2,1)S(1)}, u32[]{:S(2)}, u32[]{:S(2)}) %collective-permute-start.9) | collective-permute-done | bytes 1671200 | tf_op jit(solution)/shard_map/ppermute | solution.py:23
  551.7 30.7 %all_gather.27 = bf16[1024,128]{1,0:T(8,128)(2,1)S(1)} all-gather(bf16[128,128]{1,0:T(8,128)(2,1)S(1)} %copy-done.176), channel_id=1, replica_groups=mesh['dp'=8,'tensor'=4] {'dp'}, dimensions={0}, use_global_device_ids=true | all-gather | bytes 294912 | tf_op jit(solution)/shard_map/all_gather | solution.py:126
  603.7 16.5 collective-permute-done.12
  632.4 17.4 multiply_convert_fusion
  656.6 62.4 %reduce-scatter.14.cloned.1.call-done = f32[3264,128]{1,0:T(8,128)} async-done(((f32[3264,512]{1,0:T(8,128)}), f32[3264,128]{1,0:T(8,128)}) %reduce-scatter.14.cloned.1.call-update) | async-done | bytes 1671184 | tf_op jit(solution)/shard_map/reduce_scatter | solution.py:38
  760.9 17.0 collective-permute-done.15
  804.3 63.8 %reduce-scatter.16.cloned.1.call-done = f32[3264,128]{1,0:T(8,128)} async-done(((f32[3264,512]{1,0:T(8,128)}), f32[3264,128]{1,0:T(8,128)}) %reduce-scatter.16.cloned.1.call-update) | async-done | bytes 1671184 | tf_op jit(solution)/shard_map/reduce_scatter | solution.py:38
  922.3 105.5 %reduce-scatter.18.cloned.1.call-done = f32[6528,128]{1,0:T(8,128)} async-done(((f32[6528,512]{1,0:T(8,128)}), f32[6528,128]{1,0:T(8,128)}) %reduce-scatter.18.cloned.1.call-update) | async-done | bytes 3342352 | tf_op jit(solution)/shard_map/reduce_scatter | solution.py:38
  1062.2 25.9 %reduce-scatter.20.cloned.1.call-done = f32[476,128]{1,0:T(8,128)} async-done(((f32[476,512]{1,0:T(8,128)}), f32[476,128]{1,0:T(8,128)}) %reduce-scatter.20.cloned.1.call-update) | async-done | bytes 243728 | tf_op jit(solution)/shard_map/reduce_scatter | solution.py:38
  1110.6 17.5 reshape.245
  1147.2 17.1 fusion.61
  1164.3 30.2 %reshape.243 = f32[4,68,34816]{2,1,0:T(8,128)} reshape(f32[272,34816]{1,0:T(8,128)} %fusion.61) | data formatting | bytes 75759616 | tf_op jit(solution)/shard_map/reshape | solution.py:218
  1256.1 22.5 reduce-scatter.22.cloned.1.call-done
  1354.9 15.0 fusion.60
  1370.7 22.1 all-reduce.121
  1395.0 39.1 %reduce-scatter.24.cloned.1.call-done = f32[3264,128]{1,0:T(8,128)} async-done(((f32[3264,512]{1,0:T(8,128)}), f32[3264,128]{1,0:T(8,128)}) %reduce-scatter.24.cloned.1.call-update) | async-done | bytes 1671184 | tf_op jit(solution)/shard_map/reduce_scatter | solution.py:38
  1442.7 97.6 %all-reduce.133.cloned.1.call-done = (f32[512,512]{1,0:T(8,128)}, f32[512,512]{1,0:T(8,128)}) async-done(((f32[512,512]{1,0:T(8,128)}, f32[512,512]{1,0:T(8,128)}), (f32[512,512]{1,0:T(8,128)}, f32[512,512]{1,0:T(8,128)})) %all-reduce.133.cloned.1.call-update) | async-done | bytes 2097168 | tf_op jit(solution)/shard_map/psum | solution.py:256
  1540.4 65.4 %reduce-scatter.38.cloned.1.call-done = f32[128,128]{1,0:T(8,128)} async-done(((f32[1024,128]{1,0:T(8,128)}), f32[128,128]{1,0:T(8,128)}) %reduce-scatter.38.cloned.1.call-update) | async-done | bytes 65552 | tf_op jit(solution)/shard_map/reduce_scatter | solution.py:243
  1605.8 78.3 %reduce-scatter.30.cloned.1.call-done = f32[64,12,128]{2,0,1:T(8,128)} async-done(((f32[512,12,128]{2,0,1:T(8,128)}), f32[64,12,128]{2,0,1:T(8,128)}) %reduce-scatter.30.cloned.1.call-update) | async-done | bytes 393232 | tf_op jit(solution)/shard_map/reduce_scatter | solution.py:239
  1684.1 78.3 %reduce-scatter.26.cloned.1.call-done = f32[768,128]{1,0:T(8,128)} async-done(((f32[6144,128]{1,0:T(8,128)}), f32[768,128]{1,0:T(8,128)}) %reduce-scatter.26.cloned.1.call-update) | async-done | bytes 393232 | tf_op jit(solution)/shard_map/reduce_scatter | solution.py:237
  1762.5 91.7 %reduce-scatter.32.cloned.1.call-done = f32[1024,128]{1,0:T(8,128)} async-done(((f32[8192,128]{1,0:T(8,128)}), f32[1024,128]{1,0:T(8,128)}) %reduce-scatter.32.cloned.1.call-update) | async-done | bytes 524304 | tf_op jit(solution)/shard_map/reduce_scatter | solution.py:240
  1854.2 222.1 %reduce-scatter.34.cloned.1.call-done = f32[3264,128]{1,0:T(8,128)} async-done(((f32[26112,128]{1,0:T(8,128)}), f32[3264,128]{1,0:T(8,128)}) %reduce-scatter.34.cloned.1.call-update) | async-done | bytes 1671184 | tf_op jit(solution)/shard_map/reduce_scatter | solution.py:241
  2076.3 302.3 %reduce-scatter.28.cloned.1.call-done = f32[4352,128]{1,0:T(8,128)} async-done(((f32[34816,128]{1,0:T(8,128)}), f32[4352,128]{1,0:T(8,128)}) %reduce-scatter.28.cloned.1.call-update) | async-done | bytes 2228240 | tf_op jit(solution)/shard_map/reduce_scatter | solution.py:238
  (859 shorter events, 854.2 us)
Async XLA Ops:
  7.2 49.9 %all-gather.7.cloned.1.call-start = ((), (), s32[]{:S(2)}) async-start(), calls=%async_computation.13 | async-start | bytes 1769472 | tf_op jit(solution)/shard_map/all_gather | solution.py:120
  7.9 99.5 %all-gather.9.cloned.1.call-start = ((), (), s32[]{:S(2)}) async-start(), calls=%async_computation.14 | async-start | bytes 2359296 | tf_op jit(solution)/shard_map/all_gather | solution.py:123
  8.7 433.3 %all-gather.13.cloned.1.call-start = ((), (), s32[]{:S(2)}) async-start(), calls=%async_computation.16 | async-start | bytes 7520256 | tf_op jit(solution)/shard_map/all_gather | solution.py:124
  9.4 441.9 %all-gather.11.cloned.1.call-start = ((), (), s32[]{:S(2)}) async-start(), calls=%async_computation.15 | async-start | bytes 10027008 | tf_op jit(solution)/shard_map/all_gather | solution.py:121
  10.0 463.5 %all-gather.15.cloned.1.call-start = ((), (), s32[]{:S(2)}) async-start(), calls=%async_computation.17 | async-start | bytes 1769472 | tf_op jit(solution)/shard_map/all_gather | solution.py:122
  10.5 22.3 collective-permute-start.1
  12.6 472.1 %all-gather.17.cloned.1.call-start = ((), (), s32[]{:S(2)}) async-start(), calls=%async_computation.18 | async-start | bytes 2359296 | tf_op jit(solution)/shard_map/all_gather | solution.py:125
  113.6 605.3 %reduce-scatter.14.cloned.1.call-start = ((), (), s32[]{:S(2)}) async-start(), calls=%async_computation.19 | async-start | bytes 8355840 | tf_op jit(solution)/shard_map/reduce_scatter | solution.py:38
  512.9 36.2 %collective-permute-start.9 = (bf16[6528,128]{1,0:T(8,128)(2,1)S(1)}, bf16[6528,128]{1,0:T(8,128)(2,1)S(1)}, u32[]{:S(2)}, u32[]{:S(2)}) collective-permute-start(bf16[6528,128]{1,0:T(8,128)(2,1)S(1)} %get-tuple-element.284), channel_id=1, source_target_pairs={{0,1},{1,2},{2,3},{3,0},{4,5},{5,6},{6,7},{7,4},{8,9},{9,10},{10,1... | collective-permute-start | bytes 5013512 | tf_op jit(solution)/shard_map/ppermute | solution.py:23
  513.7 69.1 %collective-permute-start.10 = (bf16[6528,128]{1,0:T(8,128)(2,1)S(1)}, bf16[6528,128]{1,0:T(8,128)(2,1)S(1)}, u32[]{:S(2)}, u32[]{:S(2)}) collective-permute-start(bf16[6528,128]{1,0:T(8,128)(2,1)S(1)} %get-tuple-element.284), channel_id=1, source_target_pairs={{0,3},{1,0},{2,1},{3,2},{4,7},{5,4},{6,5},{7,6},{8,11},{9,8},{10,9... | collective-permute-start | bytes 5013512 | tf_op jit(solution)/shard_map/ppermute | solution.py:26
  549.2 34.1 %collective-permute-start.11 = (bf16[6528,128]{1,0:T(8,128)(2,1)S(1)}, bf16[6528,128]{1,0:T(8,128)(2,1)S(1)}, u32[]{:S(2)}, u32[]{:S(2)}) collective-permute-start(bf16[6528,128]{1,0:T(8,128)(2,1)S(1)} %collective-permute-done.9), channel_id=1, source_target_pairs={{0,1},{1,2},{2,3},{3,0},{4,5},{5,6},{6,7},{7,4},{8,9},{9,10},{10,1... | collective-permute-start | bytes 5013512 | tf_op jit(solution)/shard_map/ppermute | solution.py:23
  656.3 211.8 %reduce-scatter.16.cloned.1.call-start = ((), (), s32[]{:S(2)}) async-start(), calls=%async_computation.20 | async-start | bytes 8355840 | tf_op jit(solution)/shard_map/reduce_scatter | solution.py:38
  804.3 223.5 %reduce-scatter.18.cloned.1.call-start = ((), (), s32[]{:S(2)}) async-start(), calls=%async_computation.21 | async-start | bytes 16711680 | tf_op jit(solution)/shard_map/reduce_scatter | solution.py:38
  922.2 165.8 %reduce-scatter.20.cloned.1.call-start = ((), (), s32[]{:S(2)}) async-start(), calls=%async_computation.22 | async-start | bytes 1228800 | tf_op jit(solution)/shard_map/reduce_scatter | solution.py:38
  1062.2 216.3 %reduce-scatter.22.cloned.1.call-start = ((), (), s32[]{:S(2)}) async-start(), calls=%async_computation.23 | async-start | bytes 1228800 | tf_op jit(solution)/shard_map/reduce_scatter | solution.py:38
  1252.7 140.1 %reduce-scatter.36.cloned.1.call-start = ((), (), s32[]{:S(2)}) async-start(), calls=%async_computation.30 | async-start | bytes 4718592 | tf_op jit(solution)/shard_map/reduce_scatter | solution.py:242
  1255.8 178.3 %reduce-scatter.24.cloned.1.call-start = ((), (), s32[]{:S(2)}) async-start(), calls=%async_computation.24 | async-start | bytes 8355840 | tf_op jit(solution)/shard_map/reduce_scatter | solution.py:38
  1313.2 227.1 %all-reduce.133.cloned.1.call-start = ((), (), s32[]{:S(2)}) async-start(), calls=%async_computation.32 | async-start | bytes 4194304 | tf_op jit(solution)/shard_map/psum | solution.py:256
  1322.3 283.5 %reduce-scatter.38.cloned.1.call-start = ((), (), s32[]{:S(2)}) async-start(), calls=%async_computation.31 | async-start | bytes 589824 | tf_op jit(solution)/shard_map/reduce_scatter | solution.py:243
  1328.3 355.8 %reduce-scatter.30.cloned.1.call-start = ((), (), s32[]{:S(2)}) async-start(), calls=%async_computation.27 | async-start | bytes 3538944 | tf_op jit(solution)/shard_map/reduce_scatter | solution.py:239
  1331.1 431.3 %reduce-scatter.26.cloned.1.call-start = ((), (), s32[]{:S(2)}) async-start(), calls=%async_computation.25 | async-start | bytes 3538944 | tf_op jit(solution)/shard_map/reduce_scatter | solution.py:237
  1336.3 517.8 %reduce-scatter.32.cloned.1.call-start = ((), (), s32[]{:S(2)}) async-start(), calls=%async_computation.28 | async-start | bytes 4718592 | tf_op jit(solution)/shard_map/reduce_scatter | solution.py:240
  1342.0 734.3 %reduce-scatter.34.cloned.1.call-start = ((), (), s32[]{:S(2)}) async-start(), calls=%async_computation.29 | async-start | bytes 15040512 | tf_op jit(solution)/shard_map/reduce_scatter | solution.py:241
  1354.8 1023.8 %reduce-scatter.28.cloned.1.call-start = ((), (), s32[]{:S(2)}) async-start(), calls=%async_computation.26 | async-start | bytes 20054016 | tf_op jit(solution)/shard_map/reduce_scatter | solution.py:238
  (210 other events, 8860.7 us)
Sparse Core Ops, SparseCore 0:
  10.2 46.8 all-gather.6
  59.3 48.0 all-gather.8
  109.6 102.3 all-gather.12
  214.1 129.7 all-gather.10
  345.9 42.3 all-gather.14
  390.3 48.0 all-gather.16
  656.4 62.4 reduce-scatter.13
  804.4 63.7 reduce-scatter.15
  922.4 105.4 reduce-scatter.17
  1062.3 25.7 reduce-scatter.19
  1252.8 25.6 reduce-scatter.21
  1282.0 88.4 reduce-scatter.35
  1373.2 60.8 reduce-scatter.23
  1438.2 102.0 all-reduce.132
  1544.1 61.6 reduce-scatter.37
  1610.3 73.8 reduce-scatter.29
  1688.6 73.8 reduce-scatter.25
  1767.0 87.1 reduce-scatter.31
  1858.4 217.8 reduce-scatter.33
  2081.2 297.3 reduce-scatter.27
